TPU v7x, 32 devices: a whole 2x2x4 slice. The times are simulated.
32 devices in a mesh: blocks: 8 (over z, x), gz: 4 (over y, core).
Axes of the slice: x: 2, y: 2, z: 4, core: 2. Of those that a mesh axis runs over, the one named last changes fastest.
Arguments:
- coarse_field: float32 [4, 128, 3, 4096], P('gz', 'blocks'), may hold values from -6 to 6
- coarse_velocity: float32 [4, 128, 3, 4096], P('gz', 'blocks'), may hold values from -15 to 15
- fine_field: float32 [4, 96, 3, 4096], P('gz', 'blocks'), may hold values from -6 to 6
- fine_velocity: float32 [4, 96, 3, 4096], P('gz', 'blocks'), may hold values from -15 to 15
- pairs: int32 [4, 32, 6], P('gz', 'blocks'), may hold values from 0 to 15, as said below
Outputs:
- coarse_new: float32 [4, 128, 3, 4096], P('gz', 'blocks')
- fine_new: float32 [4, 96, 3, 4096], P('gz', 'blocks')
- face_jump: float32 [4, 32, 256], P('gz', 'blocks')
Inputs may be any that keep to these rules, and one draw needn't show every extreme that they name: `pairs`: Columns: fine slot below 12, face axis 0 to 2, owner device below 8, coarse slot below 16, quadrant row and column 0 or 1. No two rows of a device name the same fine slot and face axis, and no two rows of a group name the same coarse block, face axis and quadrant. The rows of one device name one owner device at most 2 times, and exactly 2 times for some owner; rows of one device that name the same owner differ in face axis; some owner is named 2 times by every device of its group. Each face axis stands in 1 to 2 of a device's rows.
All inputs are finite; a program needn't handle non-finite values.
Results may differ from a plain program's by a relative error of at most 0.0003.
Values sent between devices are 32-bit elements; how exact they have to be, the bound alone decides.
A program may use at most 256 MiB of HBM per device.

v0:
```python
import functools

import jax
import jax.numpy as jnp
from jax import lax
from jax.experimental import pallas as pl
from jax.experimental.pallas import tpu as pltpu
from jax.sharding import PartitionSpec as P

EDGE = 16
HALF = 8
CAP = 2
LANES = 128
ROWS = 8
TILES = EDGE**3 // LANES
BIG = 1e30
EMPTY = 3e38
TANGENT = ((1, 2), (0, 2), (0, 1))
MESH = pl.DeviceIdType.MESH


def take(values, index):
    return jnp.take_along_axis(values, index, axis=1, mode="promise_in_bounds")


def kernel(
    peers,
    groups,
    coarse_count,
    fine_count,
    pair_count,
    pairs,
    cb_hbm,
    cv_hbm,
    fb_hbm,
    fv_hbm,
    curl_c,
    curl_f,
    step_out,
    jump_out,
    cb,
    cv,
    fb,
    fv,
    emf_c,
    emf_f,
    tab_r,
    tab_n,
    rep,
    own,
    picked,
    send1,
    recv1,
    send2,
    recv2,
    gmax,
    gmax_in,
    load_sem,
    s1_sem,
    r1_sem,
    s2_sem,
    r2_sem,
    sg_sem,
    rg_sem,
):
    me = lax.axis_index("blocks")
    mg = lax.axis_index("gz")
    few = peers <= 8

    def each_peer(body):
        lax.fori_loop(1, peers, lambda k, _: (body(lax.rem(me + k, peers)), 0)[1], 0, unroll=few)

    def each_group(body):
        for k in range(1, groups):
            body(lax.rem(mg + k, groups))

    loads = [
        pltpu.make_async_copy(src, dst, load_sem.at[n])
        for n, (src, dst) in enumerate(((fb_hbm, fb), (fv_hbm, fv), (cb_hbm, cb), (cv_hbm, cv)))
    ]
    for load in loads:
        load.start()
    barrier = pltpu.get_barrier_semaphore()
    each_peer(
        lambda p: pl.semaphore_signal(barrier, inc=1, device_id=(p, mg), device_id_type=MESH)
    )
    each_group(
        lambda g: pl.semaphore_signal(barrier, inc=1, device_id=(me, g), device_id_type=MESH)
    )

    lane = lax.broadcasted_iota(jnp.int32, (ROWS, LANES), 1)
    sub = lax.broadcasted_iota(jnp.int32, (ROWS, LANES), 0)
    k_of = lane % EDGE
    first_y = lane < EDGE
    last_y = lane >= LANES - EDGE
    first_z = k_of == 0
    last_z = k_of == EDGE - 1

    def back_y(pair):
        low, high = pltpu.roll(pair[0], EDGE, 1), pltpu.roll(pair[1], EDGE, 1)
        return jnp.where(first_y, high, low), jnp.where(first_y, low, high)

    def ahead_y(pair):
        low, high = pltpu.roll(pair[0], LANES - EDGE, 1), pltpu.roll(pair[1], LANES - EDGE, 1)
        return jnp.where(last_y, high, low), jnp.where(last_y, low, high)

    def back_z(pair):
        return tuple(
            jnp.where(first_z, pltpu.roll(v, LANES - EDGE + 1, 1), pltpu.roll(v, 1, 1))
            for v in pair
        )

    def ahead_z(pair):
        return tuple(
            jnp.where(last_z, pltpu.roll(v, EDGE - 1, 1), pltpu.roll(v, LANES - 1, 1))
            for v in pair
        )

    def add(a, b):
        return a[0] + b[0], a[1] + b[1]

    def sub2(a, b):
        return a[0] - b[0], a[1] - b[1]

    def mul(a, b):
        return a[0] * b[0], a[1] * b[1]

    def scale(s, a):
        return s * a[0], s * a[1]

    def column(tile):
        return pl.ds(pl.multiple_of(tile * LANES, LANES), LANES)

    def blocked(ref, g):
        def read(c, i):
            return tuple(ref[c, ROWS * g : ROWS * g + ROWS, column(2 * i + h)] for h in range(2))

        return read

    def strided(ref, start):
        def read(c, i):
            return tuple(
                ref[pl.ds(start * 3 * TILES + c * TILES + 2 * i + h, ROWS, stride=3 * TILES), :]
                for h in range(2)
            )

        return read

    def blocked_put(ref, g):
        def put(c, i, pair):
            for h in range(2):
                ref[c, ROWS * g : ROWS * g + ROWS, column(2 * i + h)] = pair[h]

        return put

    def strided_put(ref, start):
        def put(c, i, pair):
            for h in range(2):
                ref[pl.ds(start * 3 * TILES + c * TILES + 2 * i + h, ROWS, stride=3 * TILES), :] = (
                    pair[h]
                )

        return put

    def cells(field, velocity, i, want_speed):
        after = lax.rem(i + 1, EDGE)
        b_x, b_y, b_z = field(0, i), field(1, i), field(2, i)
        c_x = scale(0.5, add(b_x, field(0, after)))
        c_y = scale(0.5, add(b_y, ahead_y(b_y)))
        c_z = scale(0.5, add(b_z, ahead_z(b_z)))
        v_x, v_y, v_z = velocity(0, i), velocity(1, i), velocity(2, i)
        cell_y = sub2(mul(v_x, c_z), mul(v_z, c_x))
        cell_z = sub2(mul(v_y, c_x), mul(v_x, c_y))
        part_y = scale(0.25, add(cell_y, back_z(cell_y)))
        part_z = scale(0.25, add(cell_z, back_y(cell_z)))
        if not want_speed:
            return part_y, part_z
        cell_x = sub2(mul(v_z, c_y), mul(v_y, c_z))
        part_x = scale(0.25, add(cell_x, back_y(cell_x)))
        e_x = add(part_x, back_z(part_x))
        vv = add(add(mul(v_x, v_x), mul(v_y, v_y)), mul(v_z, v_z))
        cc = add(add(mul(c_x, c_x), mul(c_y, c_y)), mul(c_z, c_z))
        speed = jnp.maximum(
            jnp.sqrt(vv[0]) + jnp.sqrt(cc[0]), jnp.sqrt(vv[1]) + jnp.sqrt(cc[1])
        )
        return part_y, part_z, e_x, speed

    def emf_pass(sources, target, best):
        starts = [cells(f, v, EDGE - 1, False) for f, v in sources]

        def step(i, carry):
            parts, top = carry
            fresh = []
            for g, (f, v) in enumerate(sources):
                part_y, part_z, e_x, speed = cells(f, v, i, True)
                put = blocked_put(target, g)
                put(0, i, e_x)
                put(1, i, add(part_y, parts[g][0]))
                put(2, i, add(part_z, parts[g][1]))
                top = jnp.maximum(top, speed)
                fresh.append((part_y, part_z))
            return fresh, top

        return lax.fori_loop(0, EDGE, step, (starts, best))[1]

    def curl_pass(emf, puts):
        def step(i, carry):
            after = lax.rem(i + 1, EDGE)
            for g, put in enumerate(puts):
                read = blocked(emf, g)
                e_x, e_y, e_z = read(0, i), read(1, i), read(2, i)
                put(0, i, sub2(sub2(ahead_y(e_z), e_z), sub2(ahead_z(e_y), e_y)))
                put(1, i, sub2(sub2(ahead_z(e_x), e_x), sub2(read(2, after), e_z)))
                put(2, i, sub2(sub2(read(1, after), e_y), sub2(ahead_y(e_x), e_x)))
            return carry

        lax.fori_loop(0, EDGE, step, 0)

    coarse_groups = coarse_count // ROWS
    fine_groups = -(-fine_count // ROWS)
    fine_starts = [min(ROWS * g, fine_count - ROWS) for g in range(fine_groups)]
    fine_rows = ROWS * fine_groups

    def fine_row(slot):
        last = ROWS * (fine_groups - 1)
        return jnp.where(slot < last, slot, slot - fine_starts[-1] + last)

    loads[0].wait()
    loads[1].wait()
    best = emf_pass([(strided(fb, s), strided(fv, s)) for s in fine_starts], emf_f, jnp.zeros((ROWS, LANES), jnp.float32))

    within = lane % 64
    row_m, col_n = within // HALF, within % HALF
    face_x = (row_m % 4) * 32 + col_n * 2
    for g in range(fine_groups):
        read = blocked(emf_f, g)
        for d in range(3):
            kept = []
            for which in range(2):
                axis = TANGENT[d][which]
                acc = jnp.zeros((ROWS, LANES), jnp.float32)
                if d == 0:
                    pair = read(axis, 0)
                    shift = EDGE if which == 0 else 1
                    for h in range(2):
                        mean = 0.5 * (pair[h] + pltpu.roll(pair[h], LANES - shift, 1))
                        acc = jnp.where(row_m // 4 == h, take(mean, face_x), acc)
                elif d == 1:
                    for m in range(HALF):
                        here = read(axis, 2 * m)[0]
                        other = read(axis, 2 * m + 1)[0] if which == 0 else pltpu.roll(here, LANES - 1, 1)
                        acc = jnp.where(row_m == m, take(0.5 * (here + other), col_n * 2), acc)
                else:
                    for m in range(HALF):
                        here = read(axis, 2 * m)
                        other = read(axis, 2 * m + 1) if which == 0 else [pltpu.roll(v, LANES - EDGE, 1) for v in here]
                        for h in range(2):
                            got = take(0.5 * (here[h] + other[h]), (col_n % 4) * 32)
                            acc = jnp.where((row_m == m) & (col_n // 4 == h), got, acc)
                kept.append(acc)
            tab_r[d * fine_rows + ROWS * g : d * fine_rows + ROWS * g + ROWS, :] = jnp.where(
                lane < 64, kept[0], kept[1]
            )

    slot_of = [pairs[r, 0] for r in range(pair_count)]
    face_of = [pairs[r, 1] for r in range(pair_count)]
    owner_of = [pairs[r, 2] for r in range(pair_count)]
    table_row = [face_of[r] * fine_rows + fine_row(slot_of[r]) for r in range(pair_count)]
    message_row = []
    for r in range(pair_count):
        rank = jnp.int32(0)
        for q in range(r):
            rank = rank + jnp.where(owner_of[q] == owner_of[r], 1, 0)
        message_row.append(owner_of[r] * ROWS + rank)

    box = lax.broadcasted_iota(jnp.int32, (peers * ROWS, LANES), 0)
    message = jnp.full((peers * ROWS, LANES), -1.0, jnp.float32)
    for r in range(pair_count):
        code = pairs[r, 3] * 12 + face_of[r] * 4 + pairs[r, 4] * 2 + pairs[r, 5]
        values = tab_r[pl.ds(table_row[r], 1), :]
        message = jnp.where(box == message_row[r], values, message)
        message = jnp.where(box == message_row[r] + CAP, code.astype(jnp.float32), message)
    send1[...] = message

    pl.semaphore_wait(barrier, peers - 1 + groups - 1)

    def slot(ref, p):
        return ref.at[pl.ds(pl.multiple_of(p * ROWS, ROWS), ROWS)]

    def out1(p):
        return pltpu.make_async_remote_copy(
            src_ref=slot(send1, p), dst_ref=slot(recv1, me), send_sem=s1_sem.at[p],
            recv_sem=r1_sem.at[me], device_id=(p, mg), device_id_type=MESH,
        )

    def in1(p):
        return pltpu.make_async_remote_copy(
            src_ref=slot(send1, p), dst_ref=slot(recv1, p), send_sem=s1_sem.at[p],
            recv_sem=r1_sem.at[p], device_id=(p, mg), device_id_type=MESH,
        )

    def out2(p):
        return pltpu.make_async_remote_copy(
            src_ref=slot(send2, p), dst_ref=slot(recv2, me), send_sem=s2_sem.at[p],
            recv_sem=r2_sem.at[me], device_id=(p, mg), device_id_type=MESH,
        )

    def in2(p):
        return pltpu.make_async_remote_copy(
            src_ref=slot(send2, p), dst_ref=slot(recv2, p), send_sem=s2_sem.at[p],
            recv_sem=r2_sem.at[p], device_id=(p, mg), device_id_type=MESH,
        )

    def outg(g):
        return pltpu.make_async_remote_copy(
            src_ref=gmax, dst_ref=slot(gmax_in, mg), send_sem=sg_sem.at[g],
            recv_sem=rg_sem.at[mg], device_id=(me, g), device_id_type=MESH,
        )

    def ing(g):
        return pltpu.make_async_remote_copy(
            src_ref=gmax, dst_ref=slot(gmax_in, g), send_sem=sg_sem.at[g],
            recv_sem=rg_sem.at[g], device_id=(me, g), device_id_type=MESH,
        )

    each_peer(lambda p: out1(p).start())

    loads[2].wait()
    loads[3].wait()
    best = emf_pass([(blocked(cb, g), blocked(cv, g)) for g in range(coarse_groups)], emf_c, best)
    gmax[...] = best
    each_group(lambda g: outg(g).start())

    curl_pass(emf_f, [strided_put(curl_f, s) for s in fine_starts])

    slot(recv1, me)[...] = slot(send1, me)[...]
    each_peer(lambda p: in1(p).wait_recv())
    codes = [
        [((sub + ROWS * g) * 12 + dq).astype(jnp.float32) for dq in range(12)]
        for g in range(coarse_groups)
    ]

    def row_of(ref, n):
        return jnp.broadcast_to(ref[pl.ds(n, 1), :], (ROWS, LANES))

    def collect(p, held):
        for c in range(CAP):
            values, key = row_of(recv1, p * ROWS + c), row_of(recv1, p * ROWS + CAP + c)
            held = [
                [jnp.where(key == codes[g][dq], values, held[g][dq]) for dq in range(12)]
                for g in range(coarse_groups)
            ]
        return held

    empty = jnp.full((ROWS, LANES), EMPTY, jnp.float32)
    held = lax.fori_loop(0, peers, collect, [[empty] * 12 for _ in range(coarse_groups)])
    halves = k_of < HALF
    for g in range(coarse_groups):
        def patch(axis, tile, value, mask):
            where = (axis, slice(ROWS * g, ROWS * g + ROWS), slice(tile * LANES, tile * LANES + LANES))
            put = value < BIG
            if mask is not None:
                put = put & mask
            emf_c[where] = jnp.where(put, value, emf_c[where])

        for d in range(3):
            for which in range(2):
                axis = TANGENT[d][which]
                for q1 in range(2):
                    low, high = held[g][d * 4 + q1 * 2], held[g][d * 4 + q1 * 2 + 1]
                    if d < 2:
                        spread = (lane // EDGE) * HALF + lane % HALF + 64 * which
                        both = jnp.where(halves, take(low, spread), take(high, spread))
                        if d == 0:
                            patch(axis, q1, both, None)
                        else:
                            for m in range(HALF):
                                turned = both if m == 0 else pltpu.roll(both, LANES - EDGE * m, 1)
                                patch(axis, 2 * (q1 * HALF + m), turned, first_y)
                    else:
                        for m in range(HALF):
                            for q2 in range(2):
                                got = take((low, high)[q2], m * HALF + lane // EDGE + 64 * which)
                                patch(axis, 2 * (q1 * HALF + m) + q2, got, first_z)

    curl_pass(emf_c, [blocked_put(curl_c, g) for g in range(coarse_groups)])

    def gathered_rows(read, d, h):
        out = jnp.zeros((ROWS, LANES), jnp.float32)
        for m in range(HALF):
            here = read(d, h * HALF + m)[0]
            out = jnp.where(lane // EDGE == m, here if m == 0 else pltpu.roll(here, EDGE * m, 1), out)
        return out

    for g in range(coarse_groups):
        reads = (blocked(cb, g), blocked(curl_c, g))
        for d in range(3):
            for q1 in range(2):
                if d == 0:
                    faces = [read(0, 0)[q1] for read in reads]
                elif d == 1:
                    faces = [gathered_rows(read, 1, q1) for read in reads]
                for q2 in range(2):
                    if d < 2:
                        index = row_m * EDGE + q2 * HALF + col_n
                        quads = [take(face, index) for face in faces]
                    else:
                        quads = []
                        for read in reads:
                            acc = jnp.zeros((ROWS, LANES), jnp.float32)
                            for m in range(HALF):
                                acc = jnp.where(
                                    row_m == m, take(read(2, q1 * HALF + m)[q2], col_n * EDGE), acc
                                )
                            quads.append(acc)
                    rep[(g * 12 + d * 4 + q1 * 2 + q2) * ROWS : (g * 12 + d * 4 + q1 * 2 + q2 + 1) * ROWS, :] = (
                        jnp.where(lane < 64, quads[0], quads[1])
                    )

    each_group(lambda g: ing(g).wait_recv())
    for k in range(1, groups):
        best = jnp.maximum(best, slot(gmax_in, lax.rem(mg + k, groups))[...])
    top_row = jnp.max(best, axis=0, keepdims=True)

    def answer(p, carry):
        rows = jnp.broadcast_to(top_row, (ROWS, LANES))
        for c in range(CAP):
            key = row_of(recv1, p * ROWS + CAP + c)
            acc = jnp.zeros((ROWS, LANES), jnp.float32)
            for g in range(coarse_groups):
                for dq in range(12):
                    acc = jnp.where(
                        key == codes[g][dq],
                        rep[(g * 12 + dq) * ROWS : (g * 12 + dq + 1) * ROWS, :],
                        acc,
                    )
            rows = jnp.where(sub == c, jnp.sum(acc, axis=0, keepdims=True), rows)
        slot(send2, p)[...] = rows
        return carry

    lax.fori_loop(0, peers, answer, 0)
    each_peer(lambda p: out2(p).start())

    for g in range(fine_groups):
        for n, read in enumerate((strided(fb, fine_starts[g]), strided(curl_f, fine_starts[g]))):
            for d in range(3):
                for h in range(2):
                    if d == 0:
                        face = read(0, 0)[h]
                    elif d == 1:
                        face = gathered_rows(read, 1, h)
                    else:
                        face = jnp.zeros((ROWS, LANES), jnp.float32)
                        for m in range(HALF):
                            pair = read(2, h * HALF + m)
                            for part in range(2):
                                face = jnp.where(
                                    (lane // EDGE == m) & (k_of // HALF == part),
                                    take(pair[part], (lane % HALF) * EDGE),
                                    face,
                                )
                    tab_n[
                        d * fine_rows + ROWS * g : d * fine_rows + ROWS * g + ROWS,
                        (2 * n + h) * LANES : (2 * n + h + 1) * LANES,
                    ] = face
    for r in range(pair_count):
        picked[r : r + 1, :] = tab_n[pl.ds(table_row[r], 1), :]

    slot(recv2, me)[...] = slot(send2, me)[...]
    each_peer(lambda p: in2(p).wait_recv())
    top = jnp.full((ROWS, LANES), 0.0, jnp.float32)
    top = lax.fori_loop(0, peers, lambda p, t: jnp.maximum(t, row_of(recv2, p * ROWS + CAP)), top)
    dt = 0.2 / jnp.max(top, axis=1, keepdims=True)
    step_out[...] = jnp.broadcast_to(dt, (ROWS, LANES))
    for r in range(pair_count):
        own[r : r + 1, :] = recv2[pl.ds(message_row[r], 1), :]
    for s in range(0, pair_count, ROWS):
        take_rows = min(ROWS, pair_count - s)
        quad = own[s : s + ROWS, :]
        quad = quad - dt * pltpu.roll(quad, 64, 1)
        for h in range(2):
            coarse = take(quad, (4 * h + lane // 32) * HALF + k_of // 2)
            fine = picked[s : s + ROWS, h * LANES : (h + 1) * LANES] - (dt / 0.5) * picked[
                s : s + ROWS, (2 + h) * LANES : (3 + h) * LANES
            ]
            jump_out[s : s + take_rows, h * LANES : (h + 1) * LANES] = (fine - coarse)[:take_rows]

    each_peer(lambda p: out1(p).wait_send())
    each_peer(lambda p: out2(p).wait_send())
    each_group(lambda g: outg(g).wait_send())


def on_device(peers, groups, coarse_field, coarse_velocity, fine_field, fine_velocity, pairs):
    coarse_count, fine_count = coarse_field.shape[1], fine_field.shape[1]
    pair_count = pairs.shape[1]
    cells = EDGE**3
    flat_rows = fine_count * 3 * TILES

    def coarse_view(x):
        return jnp.transpose(x[0], (1, 0, 2))

    def fine_view(x):
        return x.reshape(flat_rows, LANES)

    fine_rows = ROWS * -(-fine_count // ROWS)
    pair_rows = ROWS * -(-pair_count // ROWS)
    cb, cv = coarse_view(coarse_field), coarse_view(coarse_velocity)
    fb, fv = fine_view(fine_field), fine_view(fine_velocity)
    f32 = jnp.float32
    dma = pltpu.SemaphoreType.DMA
    vmem = pltpu.VMEM
    anywhere = pl.BlockSpec(memory_space=pl.ANY)
    inside = pl.BlockSpec(memory_space=pltpu.VMEM)
    coarse_shape, fine_shape = (3, coarse_count, cells), (flat_rows, LANES)
    curl_c, curl_f, step, jump = pl.pallas_call(
        functools.partial(kernel, peers, groups, coarse_count, fine_count, pair_count),
        out_shape=(
            jax.ShapeDtypeStruct(coarse_shape, f32),
            jax.ShapeDtypeStruct(fine_shape, f32),
            jax.ShapeDtypeStruct((ROWS, LANES), f32),
            jax.ShapeDtypeStruct((pair_count, EDGE * EDGE), f32),
        ),
        in_specs=[pl.BlockSpec(memory_space=pltpu.SMEM)] + [anywhere] * 4,
        out_specs=(inside,) * 4,
        scratch_shapes=[
            vmem(coarse_shape, f32),
            vmem(coarse_shape, f32),
            vmem(fine_shape, f32),
            vmem(fine_shape, f32),
            vmem(coarse_shape, f32),
            vmem((3, fine_rows, cells), f32),
            vmem((3 * fine_rows, LANES), f32),
            vmem((3 * fine_rows, 4 * LANES), f32),
            vmem((12 * coarse_count, LANES), f32),
            vmem((pair_rows, LANES), f32),
            vmem((pair_rows, 4 * LANES), f32),
            vmem((peers * ROWS, LANES), f32),
            vmem((peers * ROWS, LANES), f32),
            vmem((peers * ROWS, LANES), f32),
            vmem((peers * ROWS, LANES), f32),
            vmem((ROWS, LANES), f32),
            vmem((groups * ROWS, LANES), f32),
            dma((4,)),
            dma((peers,)),
            dma((peers,)),
            dma((peers,)),
            dma((peers,)),
            dma((groups,)),
            dma((groups,)),
        ],
        compiler_params=pltpu.CompilerParams(
            collective_id=0, has_side_effects=True, vmem_limit_bytes=32 * 1024 * 1024
        ),
    )(pairs[0], cb, cv, fb, fv)
    dt = step[0, 0]
    coarse_out = cb - dt * curl_c
    fine_out = fb - (dt / 0.5) * curl_f
    return (
        jnp.transpose(coarse_out, (1, 0, 2))[None],
        fine_out.reshape(1, fine_count, 3, cells),
        jump[None],
    )


def solution(mesh):
    spec = P("gz", "blocks", None, None)
    flat = P("gz", "blocks", None)
    return jax.shard_map(
        functools.partial(on_device, mesh.shape["blocks"], mesh.shape["gz"]),
        mesh=mesh,
        in_specs=(spec, spec, spec, spec, flat),
        out_specs=(spec, spec, flat),
        check_vma=False,
    )
```

profile of v0, /device:TPU:0, one launch (start us, length us, event | category | flops | bytes accessed | tf_op | source)
XLA Modules:
  0.0 33.4 jit_solution(18016878553586906954)
XLA Ops:
  0.6 0.0 copy-start.6
  0.6 0.7 %copy-done.6 = s32[1,4,6]{2,1,0:T(4,128)S(1)} copy-done((s32[1,4,6]{2,1,0:T(4,128)S(1)}, s32[1,4,6]{2,1,0:T(4,128)}, u32[]{:S(2)}) %copy-start.6) | copy-done | bytes 120
  1.3 0.0 copy-start
  1.3 1.1 %copy-done = f32[1,16,3,4096]{3,1,2,0:T(8,128)S(1)} copy-done((f32[1,16,3,4096]{3,1,2,0:T(8,128)S(1)}, f32[1,16,3,4096]{3,1,2,0:T(8,128)}, u32[]{:S(2)}) %copy-start) | copy-done | bytes 786456
  2.4 0.0 copy-start.2
  2.5 1.1 %copy-done.2 = f32[1,12,3,4096]{3,0,2,1:T(1,128)S(1)} copy-done((f32[1,12,3,4096]{3,0,2,1:T(1,128)S(1)}, f32[1,12,3,4096]{3,0,2,1:T(1,128)}, u32[]{:S(2)}) %copy-start.2) | copy-done | bytes 589848
  3.5 0.0 copy-start.4
  3.5 1.1 %copy-done.4 = f32[1,16,3,4096]{3,1,2,0:T(8,128)S(1)} copy-done((f32[1,16,3,4096]{3,1,2,0:T(8,128)S(1)}, f32[1,16,3,4096]{3,1,2,0:T(8,128)}, u32[]{:S(2)}) %copy-start.4) | copy-done | bytes 786456
  4.6 0.0 copy-start.5
  4.6 1.1 %copy-done.5 = f32[1,12,3,4096]{3,0,2,1:T(1,128)S(1)} copy-done((f32[1,12,3,4096]{3,0,2,1:T(1,128)S(1)}, f32[1,12,3,4096]{3,0,2,1:T(1,128)}, u32[]{:S(2)}) %copy-start.5) | copy-done | bytes 589848
  5.7 0.0 copy-start.3
  5.7 23.0 %shard_map.76 = (f32[3,16,4096]{2,1,0:T(8,128)S(1)}, f32[1152,128]{1,0:T(8,128)S(1)}, f32[8,128]{1,0:T(8,128)S(1)}, f32[4,256]{1,0:T(4,128)S(1)}) custom-call(s32[4,6]{1,0:T(4,128)S(1)} %bitcast.23, f32[3,16,4096]{2,1,0:T(8,128)S(1)} %bitcast.17, f32[3,16,4096]{2,1,0:T(8,128)S(1)} %bitcast.20, f32[1152,128]{1,0:T(8,128)S(1)} %bitcast.18, ...), custom_call_target="tpu_custom_call" | custom-call | tf_op jit(solution)/shard_map/pallas_call | solution.py:515
  28.7 0.5 %slice.3 = f32[1,1]{1,0:T(1,128)} slice(f32[8,128]{1,0:T(8,128)S(1)} %get-tuple-element.7), slice={[0:1], [0:1]} | slice | bytes 8 | tf_op jit(solution)/shard_map/slice | solution.py:555
  29.9 0.0 copy-done.3
  29.9 0.0 copy-start.1
  29.9 0.9 %multiply_subtract_fusion = f32[1152,128]{1,0:T(8,128)} fusion(f32[1152,128]{1,0:T(8,128)S(1)} %bitcast.19, f32[1152,128]{1,0:T(8,128)S(1)} %get-tuple-element.9, f32[]{:T(128)S(6)} %div.3), kind=kLoop, calls=%fused_computation.1 | loop fusion | flops 294912 | bytes 1769476 | tf_op jit(solution)/shard_map/sub | solution.py:557
  30.8 0.5 %copy-done.1 = f32[1,16,3,4096]{3,1,2,0:T(8,128)S(1)} copy-done((f32[1,16,3,4096]{3,1,2,0:T(8,128)S(1)}, f32[1,16,3,4096]{3,1,2,0:T(8,128)}, u32[]{:S(2)}) %copy-start.1) | copy-done | bytes 786456
  31.2 1.6 %subtract_bitcast_fusion = f32[1,16,3,4096]{3,1,2,0:T(8,128)} fusion(f32[3,16,4096]{2,1,0:T(8,128)S(1)} %get-tuple-element.8, f32[]{:T(128)} %bitcast.8, f32[1,16,3,4096]{3,1,2,0:T(8,128)S(1)} %copy-done.1), kind=kLoop, calls=%fused_computation | loop fusion | flops 393216 | bytes 2359300 | tf_op jit(solution)/shard_map/broadcast_in_dim | solution.py:559
  32.8 0.6 %copy.11 = f32[1,4,256]{2,1,0:T(4,128)} copy(f32[1,4,256]{2,1,0:T(4,128)S(1)} %bitcast.22) | data formatting | bytes 8192
Async XLA Ops:
  0.6 0.7 %copy-start.6 = (s32[1,4,6]{2,1,0:T(4,128)S(1)}, s32[1,4,6]{2,1,0:T(4,128)}, u32[]{:S(2)}) copy-start(s32[1,4,6]{2,1,0:T(4,128)} %param.9) | copy-start | bytes 292
  1.3 1.1 %copy-start = (f32[1,16,3,4096]{3,1,2,0:T(8,128)S(1)}, f32[1,16,3,4096]{3,1,2,0:T(8,128)}, u32[]{:S(2)}) copy-start(f32[1,16,3,4096]{3,1,2,0:T(8,128)} %param.5) | copy-start | bytes 2359300
  2.4 1.1 %copy-start.2 = (f32[1,12,3,4096]{3,0,2,1:T(1,128)S(1)}, f32[1,12,3,4096]{3,0,2,1:T(1,128)}, u32[]{:S(2)}) copy-start(f32[1,12,3,4096]{3,0,2,1:T(1,128)} %param.7) | copy-start | bytes 1769476
  3.5 1.1 %copy-start.4 = (f32[1,16,3,4096]{3,1,2,0:T(8,128)S(1)}, f32[1,16,3,4096]{3,1,2,0:T(8,128)}, u32[]{:S(2)}) copy-start(f32[1,16,3,4096]{3,1,2,0:T(8,128)} %param.6) | copy-start | bytes 2359300
  4.6 1.1 %copy-start.5 = (f32[1,12,3,4096]{3,0,2,1:T(1,128)S(1)}, f32[1,12,3,4096]{3,0,2,1:T(1,128)}, u32[]{:S(2)}) copy-start(f32[1,12,3,4096]{3,0,2,1:T(1,128)} %param.8) | copy-start | bytes 1769476
  5.7 24.2 %copy-start.3 = (f32[1,12,3,4096]{3,0,2,1:T(1,128)S(1)}, f32[1,12,3,4096]{3,0,2,1:T(1,128)}, u32[]{:S(2)}) copy-start(f32[1,12,3,4096]{3,0,2,1:T(1,128)} %param.7) | copy-start | bytes 1769476
  29.9 1.3 %copy-start.1 = (f32[1,16,3,4096]{3,1,2,0:T(8,128)S(1)}, f32[1,16,3,4096]{3,1,2,0:T(8,128)}, u32[]{:S(2)}) copy-start(f32[1,16,3,4096]{3,1,2,0:T(8,128)} %param.5) | copy-start | bytes 2359300
where the time goes:
time: 33.8 us; the launch traced here: 33.4 us
  Pallas kernels  23 us (68%)
  local copies, waits for them, and re-layouts  6.64 us (20%)
  other arithmetic  2.48 us (7%)
  between operations  1.32 us (4%)
    pallas_call x1, Pallas kernels, on_device(): pl.pallas_call(functools.partial(kernel, peers, groups, coarse_count, fin...  23 us
    unnamed x15, local copies, waits for them, and re-layouts  6.13 us
    broadcast_in_dim x1, other arithmetic, on_device(): jnp.transpose(coarse_out, (1, 0, 2))[None]  1.6 us
    sub x1, other arithmetic, on_device(): fine_out = fb - dt / 0.5 * curl_f  0.88 us

commit v1 on v0

--- a/solution.py
+++ b/solution.py
@@ -29,15 +29,15 @@
     coarse_count,
     fine_count,
     pair_count,
-    pairs,
+    pairs_hbm,
     cb_hbm,
     cv_hbm,
     fb_hbm,
     fv_hbm,
     curl_c,
     curl_f,
-    step_out,
     jump_out,
+    pairs,
     cb,
     cv,
     fb,
@@ -78,6 +78,8 @@
         pltpu.make_async_copy(src, dst, load_sem.at[n])
         for n, (src, dst) in enumerate(((fb_hbm, fb), (fv_hbm, fv), (cb_hbm, cb), (cv_hbm, cv)))
     ]
+    listed = pltpu.make_async_copy(pairs_hbm, pairs, load_sem.at[4])
+    listed.start()
     for load in loads:
         load.start()
     barrier = pltpu.get_barrier_semaphore()
@@ -262,6 +264,7 @@
                 lane < 64, kept[0], kept[1]
             )
 
+    listed.wait()
     slot_of = [pairs[r, 0] for r in range(pair_count)]
     face_of = [pairs[r, 1] for r in range(pair_count)]
     owner_of = [pairs[r, 2] for r in range(pair_count)]
@@ -289,39 +292,25 @@
 
     def out1(p):
         return pltpu.make_async_remote_copy(
-            src_ref=slot(send1, p), dst_ref=slot(recv1, me), send_sem=s1_sem.at[p],
-            recv_sem=r1_sem.at[me], device_id=(p, mg), device_id_type=MESH,
-        )
-
-    def in1(p):
-        return pltpu.make_async_remote_copy(
-            src_ref=slot(send1, p), dst_ref=slot(recv1, p), send_sem=s1_sem.at[p],
-            recv_sem=r1_sem.at[p], device_id=(p, mg), device_id_type=MESH,
+            src_ref=slot(send1, p), dst_ref=slot(recv1, me), send_sem=s1_sem,
+            recv_sem=r1_sem, device_id=(p, mg), device_id_type=MESH,
         )
 
     def out2(p):
         return pltpu.make_async_remote_copy(
-            src_ref=slot(send2, p), dst_ref=slot(recv2, me), send_sem=s2_sem.at[p],
-            recv_sem=r2_sem.at[me], device_id=(p, mg), device_id_type=MESH,
-        )
-
-    def in2(p):
-        return pltpu.make_async_remote_copy(
-            src_ref=slot(send2, p), dst_ref=slot(recv2, p), send_sem=s2_sem.at[p],
-            recv_sem=r2_sem.at[p], device_id=(p, mg), device_id_type=MESH,
+            src_ref=slot(send2, p), dst_ref=slot(recv2, me), send_sem=s2_sem,
+            recv_sem=r2_sem, device_id=(p, mg), device_id_type=MESH,
         )
 
     def outg(g):
         return pltpu.make_async_remote_copy(
-            src_ref=gmax, dst_ref=slot(gmax_in, mg), send_sem=sg_sem.at[g],
-            recv_sem=rg_sem.at[mg], device_id=(me, g), device_id_type=MESH,
+            src_ref=gmax, dst_ref=slot(gmax_in, mg), send_sem=sg_sem,
+            recv_sem=rg_sem, device_id=(me, g), device_id_type=MESH,
         )
 
-    def ing(g):
-        return pltpu.make_async_remote_copy(
-            src_ref=gmax, dst_ref=slot(gmax_in, g), send_sem=sg_sem.at[g],
-            recv_sem=rg_sem.at[g], device_id=(me, g), device_id_type=MESH,
-        )
+    def drain(ref, sem, count):
+        part = ref.at[pl.ds(0, ROWS * count)]
+        pltpu.make_async_copy(part, part, sem).wait()
 
     each_peer(lambda p: out1(p).start())
 
@@ -333,8 +322,58 @@
 
     curl_pass(emf_f, [strided_put(curl_f, s) for s in fine_starts])
 
+
+    def gathered_rows(read, d, h):
+        out = jnp.zeros((ROWS, LANES), jnp.float32)
+        for m in range(HALF):
+            here = read(d, h * HALF + m)[0]
+            out = jnp.where(lane // EDGE == m, here if m == 0 else pltpu.roll(here, EDGE * m, 1), out)
+        return out
+
+    def normal_curl(g):
+        edge = blocked(emf_c, g)
+
+        def read(d, i):
+            after = (i + 1) % EDGE
+            if d == 0:
+                e_y, e_z = edge(1, i), edge(2, i)
+                return sub2(sub2(ahead_y(e_z), e_z), sub2(ahead_z(e_y), e_y))
+            if d == 1:
+                e_x, e_z = edge(0, i)[:1], edge(2, i)
+                return ((ahead_z(e_x)[0] - e_x[0]) - (edge(2, after)[0] - e_z[0]),)
+            e_x, e_y = edge(0, i), edge(1, i)
+            return sub2(sub2(edge(1, after), e_y), sub2(ahead_y(e_x), e_x))
+
+        return read
+
+    def quadrants(read, g, second):
+        def put(d, q1, q2, value):
+            n = (g * 12 + d * 4 + q1 * 2 + q2) * ROWS
+            if second:
+                value = jnp.where(lane < 64, rep[n : n + ROWS, :], value)
+            rep[n : n + ROWS, :] = value
+
+        plane = read(0, 0)
+        for d in range(2):
+            for q1 in range(2):
+                face = plane[q1] if d == 0 else gathered_rows(read, 1, q1)
+                for q2 in range(2):
+                    put(d, q1, q2, take(face, row_m * EDGE + q2 * HALF + col_n))
+        for q1 in range(2):
+            got = [jnp.zeros((ROWS, LANES), jnp.float32)] * 2
+            for m in range(HALF):
+                pair = read(2, q1 * HALF + m)
+                got = [
+                    jnp.where(row_m == m, take(pair[q2], col_n * EDGE), got[q2]) for q2 in range(2)
+                ]
+            for q2 in range(2):
+                put(2, q1, q2, got[q2])
+
+    for g in range(coarse_groups):
+        quadrants(blocked(cb, g), g, False)
+
     slot(recv1, me)[...] = slot(send1, me)[...]
-    each_peer(lambda p: in1(p).wait_recv())
+    drain(recv1, r1_sem, peers - 1)
     codes = [
         [((sub + ROWS * g) * 12 + dq).astype(jnp.float32) for dq in range(12)]
         for g in range(coarse_groups)
@@ -353,7 +392,7 @@
         return held
 
     empty = jnp.full((ROWS, LANES), EMPTY, jnp.float32)
-    held = lax.fori_loop(0, peers, collect, [[empty] * 12 for _ in range(coarse_groups)])
+    held = lax.fori_loop(0, peers, collect, [[empty] * 12 for _ in range(coarse_groups)], unroll=few)
     halves = k_of < HALF
     for g in range(coarse_groups):
         def patch(axis, tile, value, mask):
@@ -383,41 +422,10 @@
                                 got = take((low, high)[q2], m * HALF + lane // EDGE + 64 * which)
                                 patch(axis, 2 * (q1 * HALF + m) + q2, got, first_z)
 
-    curl_pass(emf_c, [blocked_put(curl_c, g) for g in range(coarse_groups)])
-
-    def gathered_rows(read, d, h):
-        out = jnp.zeros((ROWS, LANES), jnp.float32)
-        for m in range(HALF):
-            here = read(d, h * HALF + m)[0]
-            out = jnp.where(lane // EDGE == m, here if m == 0 else pltpu.roll(here, EDGE * m, 1), out)
-        return out
-
     for g in range(coarse_groups):
-        reads = (blocked(cb, g), blocked(curl_c, g))
-        for d in range(3):
-            for q1 in range(2):
-                if d == 0:
-                    faces = [read(0, 0)[q1] for read in reads]
-                elif d == 1:
-                    faces = [gathered_rows(read, 1, q1) for read in reads]
-                for q2 in range(2):
-                    if d < 2:
-                        index = row_m * EDGE + q2 * HALF + col_n
-                        quads = [take(face, index) for face in faces]
-                    else:
-                        quads = []
-                        for read in reads:
-                            acc = jnp.zeros((ROWS, LANES), jnp.float32)
-                            for m in range(HALF):
-                                acc = jnp.where(
-                                    row_m == m, take(read(2, q1 * HALF + m)[q2], col_n * EDGE), acc
-                                )
-                            quads.append(acc)
-                    rep[(g * 12 + d * 4 + q1 * 2 + q2) * ROWS : (g * 12 + d * 4 + q1 * 2 + q2 + 1) * ROWS, :] = (
-                        jnp.where(lane < 64, quads[0], quads[1])
-                    )
-
-    each_group(lambda g: ing(g).wait_recv())
+        quadrants(normal_curl(g), g, True)
+
+    drain(gmax_in, rg_sem, groups - 1)
     for k in range(1, groups):
         best = jnp.maximum(best, slot(gmax_in, lax.rem(mg + k, groups))[...])
     top_row = jnp.max(best, axis=0, keepdims=True)
@@ -438,8 +446,9 @@
         slot(send2, p)[...] = rows
         return carry
 
-    lax.fori_loop(0, peers, answer, 0)
+    lax.fori_loop(0, peers, answer, 0, unroll=few)
     each_peer(lambda p: out2(p).start())
+    curl_pass(emf_c, [blocked_put(curl_c, g) for g in range(coarse_groups)])
 
     for g in range(fine_groups):
         for n, read in enumerate((strided(fb, fine_starts[g]), strided(curl_f, fine_starts[g]))):
@@ -467,11 +476,10 @@
         picked[r : r + 1, :] = tab_n[pl.ds(table_row[r], 1), :]
 
     slot(recv2, me)[...] = slot(send2, me)[...]
-    each_peer(lambda p: in2(p).wait_recv())
+    drain(recv2, r2_sem, peers - 1)
     top = jnp.full((ROWS, LANES), 0.0, jnp.float32)
-    top = lax.fori_loop(0, peers, lambda p, t: jnp.maximum(t, row_of(recv2, p * ROWS + CAP)), top)
+    top = lax.fori_loop(0, peers, lambda p, t: jnp.maximum(t, row_of(recv2, p * ROWS + CAP)), top, unroll=few)
     dt = 0.2 / jnp.max(top, axis=1, keepdims=True)
-    step_out[...] = jnp.broadcast_to(dt, (ROWS, LANES))
     for r in range(pair_count):
         own[r : r + 1, :] = recv2[pl.ds(message_row[r], 1), :]
     for s in range(0, pair_count, ROWS):
@@ -485,9 +493,37 @@
             ]
             jump_out[s : s + take_rows, h * LANES : (h + 1) * LANES] = (fine - coarse)[:take_rows]
 
-    each_peer(lambda p: out1(p).wait_send())
-    each_peer(lambda p: out2(p).wait_send())
-    each_group(lambda g: outg(g).wait_send())
+    def finish(i, carry):
+        for g in range(coarse_groups):
+            read, put, curl = blocked(cb, g), blocked_put(curl_c, g), blocked(curl_c, g)
+            for c in range(3):
+                put(c, i, sub2(read(c, i), (dt * curl(c, i)[0], dt * curl(c, i)[1])))
+        return carry
+
+    lax.fori_loop(0, EDGE, finish, 0, unroll=2)
+    doubled = dt / 0.5
+    span = fine_count * 3 * ROWS
+
+    def finish_fine(n, carry):
+        part = pl.ds(pl.multiple_of(n * span, ROWS), span)
+        curl_f[part, :] = fb[part, :] - doubled[:1] * curl_f[part, :]
+        return carry
+
+    lax.fori_loop(0, TILES // ROWS, finish_fine, 0)
+    drain(send1, s1_sem, peers - 1)
+    drain(send2, s2_sem, peers - 1)
+    drain(gmax_in, sg_sem, groups - 1)
+
+
+def store(curl_c, curl_f, jump, out_c, out_f, out_j, sems):
+    copies = [
+        pltpu.make_async_copy(src, dst, sems.at[n])
+        for n, (src, dst) in enumerate(((curl_c, out_c), (curl_f, out_f), (jump, out_j)))
+    ]
+    for copy in copies:
+        copy.start()
+    for copy in copies:
+        copy.wait()
 
 
 def on_device(peers, groups, coarse_field, coarse_velocity, fine_field, fine_velocity, pairs):
@@ -506,23 +542,26 @@
     pair_rows = ROWS * -(-pair_count // ROWS)
     cb, cv = coarse_view(coarse_field), coarse_view(coarse_velocity)
     fb, fv = fine_view(fine_field), fine_view(fine_velocity)
+    operands = [
+        pltpu.with_memory_space_constraint(x, pltpu.HBM) for x in (pairs[0], cb, cv, fb, fv)
+    ]
     f32 = jnp.float32
     dma = pltpu.SemaphoreType.DMA
     vmem = pltpu.VMEM
-    anywhere = pl.BlockSpec(memory_space=pl.ANY)
+    anywhere = pl.BlockSpec(memory_space=pltpu.HBM)
     inside = pl.BlockSpec(memory_space=pltpu.VMEM)
     coarse_shape, fine_shape = (3, coarse_count, cells), (flat_rows, LANES)
-    curl_c, curl_f, step, jump = pl.pallas_call(
+    new_c, new_f, jump = pl.pallas_call(
         functools.partial(kernel, peers, groups, coarse_count, fine_count, pair_count),
         out_shape=(
             jax.ShapeDtypeStruct(coarse_shape, f32),
             jax.ShapeDtypeStruct(fine_shape, f32),
-            jax.ShapeDtypeStruct((ROWS, LANES), f32),
             jax.ShapeDtypeStruct((pair_count, EDGE * EDGE), f32),
         ),
-        in_specs=[pl.BlockSpec(memory_space=pltpu.SMEM)] + [anywhere] * 4,
-        out_specs=(inside,) * 4,
+        in_specs=[anywhere] * 5,
+        out_specs=(inside,) * 3,
         scratch_shapes=[
+            pltpu.SMEM(pairs.shape[1:], jnp.int32),
             vmem(coarse_shape, f32),
             vmem(coarse_shape, f32),
             vmem(fine_shape, f32),
@@ -540,21 +579,29 @@
             vmem((peers * ROWS, LANES), f32),
             vmem((ROWS, LANES), f32),
             vmem((groups * ROWS, LANES), f32),
-            dma((4,)),
-            dma((peers,)),
-            dma((peers,)),
-            dma((peers,)),
-            dma((peers,)),
-            dma((groups,)),
-            dma((groups,)),
+            dma((5,)),
+            dma,
+            dma,
+            dma,
+            dma,
+            dma,
+            dma,
         ],
         compiler_params=pltpu.CompilerParams(
             collective_id=0, has_side_effects=True, vmem_limit_bytes=32 * 1024 * 1024
         ),
-    )(pairs[0], cb, cv, fb, fv)
-    dt = step[0, 0]
-    coarse_out = cb - dt * curl_c
-    fine_out = fb - (dt / 0.5) * curl_f
+    )(*operands)
+    coarse_out, fine_out, jump = pl.pallas_call(
+        store,
+        out_shape=(
+            jax.ShapeDtypeStruct(coarse_shape, f32),
+            jax.ShapeDtypeStruct(fine_shape, f32),
+            jax.ShapeDtypeStruct((pair_count, EDGE * EDGE), f32),
+        ),
+        in_specs=[inside] * 3,
+        out_specs=(anywhere,) * 3,
+        scratch_shapes=[dma((3,))],
+    )(*(pltpu.with_memory_space_constraint(x, pltpu.VMEM) for x in (new_c, new_f, jump)))
     return (
         jnp.transpose(coarse_out, (1, 0, 2))[None],
         fine_out.reshape(1, fine_count, 3, cells),

time: 33.8 us -> 27.4 us (0.81)
  local copies, waits for them, and re-layouts: 6.64 us -> 0 us
  Pallas kernels: 23 us -> 26.6 us
  other arithmetic: 2.48 us -> 0 us
  between operations: 1.32 us -> 0.64 us
    unnamed x15 -> x0, local copies, waits for them, and re-layouts: 6.13 us -> none
    pallas_call x1, Pallas kernels: 23 us -> 25.5 us  [on_device(): pl.pallas_call(functools.partial(kernel, peers, groups, coarse_count, fin...]
    broadcast_in_dim x1 -> x0, other arithmetic: 1.6 us -> none  [on_device(): jnp.transpose(coarse_out, (1, 0, 2))[None]]
    pallas_call x0 -> x1, Pallas kernels: none -> 1.1 us  [on_device(): pl.pallas_call(store, out_shape=(jax.ShapeDtypeStruct(coarse_shape, f32),...]
    sub x1 -> x0, other arithmetic: 0.88 us -> none  [on_device(): fine_out = fb - dt / 0.5 * curl_f]
    slice x1 -> x0, local copies, waits for them, and re-layouts: 0.51 us -> none  [on_device(): dt = step[0, 0]]
where the time goes in v1:
time: 27.4 us; the launch traced here: 27.2 us
  Pallas kernels  26.6 us (97%)
  between operations  0.64 us (2%)
    pallas_call x1, Pallas kernels, on_device(): pl.pallas_call(functools.partial(kernel, peers, groups, coarse_count, fin...  25.5 us
    pallas_call x1, Pallas kernels, on_device(): pl.pallas_call(store, out_shape=(jax.ShapeDtypeStruct(coarse_shape, f32),...  1.1 us

profile of v1, /device:TPU:0, one launch (start us, length us, event | category | flops | bytes accessed | tf_op | source)
XLA Modules:
  0.0 27.2 jit_solution(3803413522563392163)
XLA Ops:
  0.6 25.5 %shard_map.76 = (f32[3,16,4096]{2,1,0:T(8,128)S(1)}, f32[1152,128]{1,0:T(8,128)S(1)}, f32[4,256]{1,0:T(4,128)S(1)}) custom-call(s32[4,6]{1,0:T(4,128)} %bitcast.18, f32[3,16,4096]{2,1,0:T(8,128)} %bitcast.14, f32[3,16,4096]{2,1,0:T(8,128)} %bitcast.15, f32[1152,128]{1,0:T(8,128)} %bitcast.16, f32[1152,128]{1,0:T(8,128)} %bitcast.17), custom_call_target="tpu_custom_call" | custom-call | tf_op jit(solution)/shard_map/pallas_call | solution.py:554
  26.1 1.1 %shard_map.77 = (f32[3,16,4096]{2,1,0:T(8,128)}, f32[1152,128]{1,0:T(8,128)}, f32[4,256]{1,0:T(4,128)}) custom-call(f32[3,16,4096]{2,1,0:T(8,128)S(1)} %get-tuple-element.9.curl_c, f32[1152,128]{1,0:T(8,128)S(1)} %get-tuple-element.10.curl_f, f32[4,256]{1,0:T(4,128)S(1)} %get-tuple-element.11.jump), custom_call_target="tpu_custom_call" | custom-call | tf_op jit(solution)/shard_map/pallas_call | solution.py:594

commit v2 on v1

--- a/solution.py
+++ b/solution.py
@@ -74,14 +74,28 @@
         for k in range(1, groups):
             body(lax.rem(mg + k, groups))
 
-    loads = [
-        pltpu.make_async_copy(src, dst, load_sem.at[n])
-        for n, (src, dst) in enumerate(((fb_hbm, fb), (fv_hbm, fv), (cb_hbm, cb), (cv_hbm, cv)))
-    ]
+    coarse_groups = coarse_count // ROWS
+    fine_groups = -(-fine_count // ROWS)
+    fine_starts = [min(ROWS * g, fine_count - ROWS) for g in range(fine_groups)]
+    fine_rows = ROWS * fine_groups
+    arrivals = ((fb_hbm, fb), (fv_hbm, fv), (cb_hbm, cb), (cv_hbm, cv))
     listed = pltpu.make_async_copy(pairs_hbm, pairs, load_sem.at[4])
     listed.start()
-    for load in loads:
-        load.start()
+    for n, (src, dst) in enumerate(arrivals):
+        if n >= 2:
+            pltpu.make_async_copy(src, dst, load_sem.at[n]).start()
+        else:
+            for c in range(3):
+                for g, start in enumerate(fine_starts):
+                    pltpu.make_async_copy(
+                        src.at[pl.ds(start, ROWS), c, 0],
+                        dst.at[c, pl.ds(ROWS * g, ROWS)],
+                        load_sem.at[n],
+                    ).start()
+
+    def loaded(n):
+        pltpu.make_async_copy(arrivals[n][1], arrivals[n][1], load_sem.at[n]).wait()
+
     barrier = pltpu.get_barrier_semaphore()
     each_peer(
         lambda p: pl.semaphore_signal(barrier, inc=1, device_id=(p, mg), device_id_type=MESH)
@@ -139,28 +153,10 @@
 
         return read
 
-    def strided(ref, start):
-        def read(c, i):
-            return tuple(
-                ref[pl.ds(start * 3 * TILES + c * TILES + 2 * i + h, ROWS, stride=3 * TILES), :]
-                for h in range(2)
-            )
-
-        return read
-
     def blocked_put(ref, g):
         def put(c, i, pair):
             for h in range(2):
                 ref[c, ROWS * g : ROWS * g + ROWS, column(2 * i + h)] = pair[h]
-
-        return put
-
-    def strided_put(ref, start):
-        def put(c, i, pair):
-            for h in range(2):
-                ref[pl.ds(start * 3 * TILES + c * TILES + 2 * i + h, ROWS, stride=3 * TILES), :] = (
-                    pair[h]
-                )
 
         return put
 
@@ -218,18 +214,14 @@
 
         lax.fori_loop(0, EDGE, step, 0)
 
-    coarse_groups = coarse_count // ROWS
-    fine_groups = -(-fine_count // ROWS)
-    fine_starts = [min(ROWS * g, fine_count - ROWS) for g in range(fine_groups)]
-    fine_rows = ROWS * fine_groups
 
     def fine_row(slot):
         last = ROWS * (fine_groups - 1)
         return jnp.where(slot < last, slot, slot - fine_starts[-1] + last)
 
-    loads[0].wait()
-    loads[1].wait()
-    best = emf_pass([(strided(fb, s), strided(fv, s)) for s in fine_starts], emf_f, jnp.zeros((ROWS, LANES), jnp.float32))
+    loaded(0)
+    loaded(1)
+    best = emf_pass([(blocked(fb, g), blocked(fv, g)) for g in range(fine_groups)], emf_f, jnp.zeros((ROWS, LANES), jnp.float32))
 
     within = lane % 64
     row_m, col_n = within // HALF, within % HALF
@@ -314,13 +306,13 @@
 
     each_peer(lambda p: out1(p).start())
 
-    loads[2].wait()
-    loads[3].wait()
+    loaded(2)
+    loaded(3)
     best = emf_pass([(blocked(cb, g), blocked(cv, g)) for g in range(coarse_groups)], emf_c, best)
     gmax[...] = best
     each_group(lambda g: outg(g).start())
 
-    curl_pass(emf_f, [strided_put(curl_f, s) for s in fine_starts])
+    curl_pass(emf_f, [blocked_put(curl_f, g) for g in range(fine_groups)])
 
 
     def gathered_rows(read, d, h):
@@ -451,7 +443,7 @@
     curl_pass(emf_c, [blocked_put(curl_c, g) for g in range(coarse_groups)])
 
     for g in range(fine_groups):
-        for n, read in enumerate((strided(fb, fine_starts[g]), strided(curl_f, fine_starts[g]))):
+        for n, read in enumerate((blocked(fb, g), blocked(curl_f, g))):
             for d in range(3):
                 for h in range(2):
                     if d == 0:
@@ -494,35 +486,48 @@
             jump_out[s : s + take_rows, h * LANES : (h + 1) * LANES] = (fine - coarse)[:take_rows]
 
     def finish(i, carry):
-        for g in range(coarse_groups):
-            read, put, curl = blocked(cb, g), blocked_put(curl_c, g), blocked(curl_c, g)
-            for c in range(3):
-                put(c, i, sub2(read(c, i), (dt * curl(c, i)[0], dt * curl(c, i)[1])))
+        for field, update, factor, count in (
+            (cb, curl_c, dt, coarse_groups),
+            (fb, curl_f, dt / 0.5, fine_groups),
+        ):
+            for g in range(count):
+                read, put, curl = blocked(field, g), blocked_put(update, g), blocked(update, g)
+                for c in range(3):
+                    low, high = curl(c, i)
+                    put(c, i, sub2(read(c, i), (factor * low, factor * high)))
         return carry
 
     lax.fori_loop(0, EDGE, finish, 0, unroll=2)
-    doubled = dt / 0.5
-    span = fine_count * 3 * ROWS
-
-    def finish_fine(n, carry):
-        part = pl.ds(pl.multiple_of(n * span, ROWS), span)
-        curl_f[part, :] = fb[part, :] - doubled[:1] * curl_f[part, :]
-        return carry
-
-    lax.fori_loop(0, TILES // ROWS, finish_fine, 0)
     drain(send1, s1_sem, peers - 1)
     drain(send2, s2_sem, peers - 1)
     drain(gmax_in, sg_sem, groups - 1)
 
 
-def store(curl_c, curl_f, jump, out_c, out_f, out_j, sems):
-    copies = [
-        pltpu.make_async_copy(src, dst, sems.at[n])
-        for n, (src, dst) in enumerate(((curl_c, out_c), (curl_f, out_f), (jump, out_j)))
+def store(new_c, new_f, jump, out_c, out_f, out_j, sems):
+    count = out_f.shape[0]
+    fine_groups = new_f.shape[1] // ROWS
+
+    def fine(g, c):
+        start = min(ROWS * g, count - ROWS)
+        return pltpu.make_async_copy(
+            new_f.at[c, pl.ds(ROWS * g, ROWS)],
+            out_f.at[pl.ds(start, ROWS), c, 0],
+            sems.at[2 + 3 * g + c],
+        )
+
+    last = [fine(fine_groups - 1, c) for c in range(3)]
+    rest = [
+        pltpu.make_async_copy(new_c, out_c, sems.at[0]),
+        pltpu.make_async_copy(jump, out_j, sems.at[1]),
     ]
-    for copy in copies:
+    for copy in last + rest:
         copy.start()
-    for copy in copies:
+    for copy in last:
+        copy.wait()
+    before = [fine(g, c) for g in range(fine_groups - 1) for c in range(3)]
+    for copy in before:
+        copy.start()
+    for copy in rest + before:
         copy.wait()
 
 
@@ -530,13 +535,12 @@
     coarse_count, fine_count = coarse_field.shape[1], fine_field.shape[1]
     pair_count = pairs.shape[1]
     cells = EDGE**3
-    flat_rows = fine_count * 3 * TILES
 
     def coarse_view(x):
         return jnp.transpose(x[0], (1, 0, 2))
 
     def fine_view(x):
-        return x.reshape(flat_rows, LANES)
+        return jnp.transpose(x, (1, 2, 0, 3))
 
     fine_rows = ROWS * -(-fine_count // ROWS)
     pair_rows = ROWS * -(-pair_count // ROWS)
@@ -550,7 +554,7 @@
     vmem = pltpu.VMEM
     anywhere = pl.BlockSpec(memory_space=pltpu.HBM)
     inside = pl.BlockSpec(memory_space=pltpu.VMEM)
-    coarse_shape, fine_shape = (3, coarse_count, cells), (flat_rows, LANES)
+    coarse_shape, fine_shape = (3, coarse_count, cells), (3, fine_rows, cells)
     new_c, new_f, jump = pl.pallas_call(
         functools.partial(kernel, peers, groups, coarse_count, fine_count, pair_count),
         out_shape=(
@@ -595,16 +599,16 @@
         store,
         out_shape=(
             jax.ShapeDtypeStruct(coarse_shape, f32),
-            jax.ShapeDtypeStruct(fine_shape, f32),
+            jax.ShapeDtypeStruct((fine_count, 3, 1, cells), f32),
             jax.ShapeDtypeStruct((pair_count, EDGE * EDGE), f32),
         ),
         in_specs=[inside] * 3,
         out_specs=(anywhere,) * 3,
-        scratch_shapes=[dma((3,))],
+        scratch_shapes=[dma((2 + 3 * (fine_rows // ROWS),))],
     )(*(pltpu.with_memory_space_constraint(x, pltpu.VMEM) for x in (new_c, new_f, jump)))
     return (
         jnp.transpose(coarse_out, (1, 0, 2))[None],
-        fine_out.reshape(1, fine_count, 3, cells),
+        jnp.transpose(fine_out, (2, 0, 1, 3)),
         jump[None],
     )
 

time: 27.4 us -> 28 us (1.022)
  Pallas kernels: 26.6 us -> 27.2 us
    pallas_call x1, Pallas kernels: 1.1 us -> 1.56 us  [on_device(): pl.pallas_call(store, out_shape=(jax.ShapeDtypeStruct(coarse_shape, f32),...]
where the time goes in v2:
time: 28 us; the launch traced here: 27.8 us
  Pallas kernels  27.2 us (97%)
  between operations  0.64 us (2%)
    pallas_call x1, Pallas kernels, on_device(): pl.pallas_call(functools.partial(kernel, peers, groups, coarse_count, fin...  25.6 us
    pallas_call x1, Pallas kernels, on_device(): pl.pallas_call(store, out_shape=(jax.ShapeDtypeStruct(coarse_shape, f32),...  1.56 us

profile of v2, /device:TPU:0, one launch (start us, length us, event | category | flops | bytes accessed | tf_op | source)
XLA Modules:
  0.0 27.8 jit_solution(13477222888659419671)
XLA Ops:
  0.6 25.6 %shard_map.76 = (f32[3,16,4096]{2,1,0:T(8,128)S(1)}, f32[3,16,4096]{2,1,0:T(8,128)S(1)}, f32[4,256]{1,0:T(4,128)S(1)}) custom-call(s32[4,6]{1,0:T(4,128)} %bitcast.18, f32[3,16,4096]{2,1,0:T(8,128)} %bitcast.14, f32[3,16,4096]{2,1,0:T(8,128)} %bitcast.15, f32[12,3,1,4096]{3,2,1,0:T(1,128)} %bitcast.16, f32[12,3,1,4096]{3,2,1,0:T(1,128)} %bitcast.17), custom_call_target="tpu_custom_call" | custom-call | tf_op jit(solution)/shard_map/pallas_call | solution.py:558
  26.3 1.6 %shard_map.77 = (f32[3,16,4096]{2,1,0:T(8,128)}, f32[12,3,1,4096]{3,2,1,0:T(1,128)}, f32[4,256]{1,0:T(4,128)}) custom-call(f32[3,16,4096]{2,1,0:T(8,128)S(1)} %get-tuple-element.9.new_c, f32[3,16,4096]{2,1,0:T(8,128)S(1)} %get-tuple-element.10.new_f, f32[4,256]{1,0:T(4,128)S(1)} %get-tuple-element.11.jump), custom_call_target="tpu_custom_call" | custom-call | tf_op jit(solution)/shard_map/pallas_call | solution.py:598
